TPU v7x, 32 devices: a whole 2x2x4 slice. The times are simulated.
32 devices in a mesh: ctx: 2 (over y), fsdp: 4 (over z), rep: 4 (over x, core).
Axes of the slice: x: 2, y: 2, z: 4, core: 2. Of those that a mesh axis runs over, the one named last changes fastest.
Arguments:
- tokens: bfloat16 [16, 256, 2048], P(('fsdp', 'rep'), 'ctx'), may hold values from -6 to 6
- cotangent: bfloat16 [16, 256, 2048], P(('fsdp', 'rep'), 'ctx'), may hold values from -6 to 6
- lengths: int32 [16], P(('fsdp', 'rep')), may hold values from 64 to 256, as said below
- first_gain: bfloat16 [2048], P('fsdp'), may hold values from 0.25 to 1.75
- joint_matrix: bfloat16 [2048, 1920], P('fsdp'), may hold values from -0.125 to 0.125
- query_gain: bfloat16 [64], P('fsdp'), may hold values from 0.25 to 1.75
- key_gain: bfloat16 [64], P('fsdp'), may hold values from 0.25 to 1.75
- out_weight: bfloat16 [1280, 2048], P('fsdp'), may hold values from -2 to 2
- second_gain: bfloat16 [2048], P('fsdp'), may hold values from 0.25 to 1.75
- expand_weight: bfloat16 [2048, 10240], P('fsdp'), may hold values from -0.125 to 0.125
- contract_weight: bfloat16 [5120, 2048], P('fsdp'), may hold values from -0.078125 to 0.078125
Outputs:
- layer_output: bfloat16 [16, 256, 2048], P(('fsdp', 'rep'), 'ctx')
- input_gradient: float32 [16, 256, 2048], P(('fsdp', 'rep'), 'ctx')
- first_gradient: float32 [2048], P('fsdp')
- joint_gradient: float32 [2048, 1920], P('fsdp')
- query_gradient: float32 [64], P('fsdp')
- key_gradient: float32 [64], P('fsdp')
- out_gradient: float32 [1280, 2048], P('fsdp')
- second_gradient: float32 [2048], P('fsdp')
- expand_gradient: float32 [2048, 10240], P('fsdp')
- contract_gradient: float32 [5120, 2048], P('fsdp')
Inputs may be any that keep to these rules, and one draw needn't show every extreme that they name: `lengths`: valid positions count from each slot's start; some slot is full and some slot has 64.
All inputs are finite; a program needn't handle non-finite values.
Results may differ from a plain program's by a relative error of at most 0.012.
Values may be sent and summed in bfloat16 or wider, within the bound.
No kernel may reach another device: no remote copies, remote signals or barrier semaphores. Data moves between devices by JAX's collectives and lax.ppermute only.
A program may use at most 384 MiB of HBM per device.

v0:
```python
import math
import jax
import jax.numpy as jnp
from jax import lax
from jax.sharding import PartitionSpec as P

QUERY_HEADS = 20
KEY_VALUE_HEADS = 5
HEAD_SIZE = 64
FF = 5120
epsilon = 1e-06
masked_fill_value = -1e30


def tables(positions, width):
    steps = jnp.arange(width // 2, dtype=jnp.float32)
    rates = jnp.exp(steps * (-2.0 * math.log(10000.0) / width))
    angles = positions.astype(jnp.float32)[:, None] * rates[None, :]
    return (jnp.cos(angles)[:, None, :], jnp.sin(angles)[:, None, :])


def rotate(field, cosine_table, sine_table):
    half = field.shape[-1] // 2
    first, second = (field[..., :half], field[..., half:])
    return jnp.concatenate(
        [first * cosine_table - second * sine_table, second * cosine_table + first * sine_table],
        axis=-1,
    )


def reverse_rotation(upstream, cosine_table, sine_table):
    half = upstream.shape[-1] // 2
    first, second = (upstream[..., :half], upstream[..., half:])
    return jnp.concatenate(
        [first * cosine_table + second * sine_table, second * cosine_table - first * sine_table],
        axis=-1,
    )


def rms_parts(field):
    inverse = lax.rsqrt(jnp.mean(field * field, axis=-1, keepdims=True) + epsilon)
    return (field * inverse, inverse)


def rms_back(upstream, normed, inverse):
    return inverse * (upstream - normed * jnp.mean(upstream * normed, axis=-1, keepdims=True))


def cross_product(left, right):
    return lax.dot_general(
        left, right, (((0,), (0,)), ((), ())), preferred_element_type=jnp.float32
    )


def against(left, right):
    return lax.dot_general(
        left, right, (((1,), (1,)), ((), ())), preferred_element_type=jnp.float32
    )


def block_scores(grouped_query, pair_all, start, positions, slot_length_value, stretch_factor):
    key_span_width = KEY_VALUE_HEADS * HEAD_SIZE
    block_pairing = lax.dynamic_slice_in_dim(pair_all, start, stretch_factor, 0)
    key_rows = block_pairing[:, :key_span_width].reshape(stretch_factor, KEY_VALUE_HEADS, HEAD_SIZE)
    value_rows = block_pairing[:, key_span_width:].reshape(
        stretch_factor, KEY_VALUE_HEADS, HEAD_SIZE
    )
    scores = jnp.einsum(
        "qgrd,kgd->grqk", grouped_query, key_rows, preferred_element_type=jnp.float32
    ) * HEAD_SIZE ** (-0.5)
    key_pos = start + jnp.arange(stretch_factor, dtype=jnp.int32)
    allowed = (key_pos[None, :] <= positions[:, None]) & (key_pos[None, :] < slot_length_value)
    scores = jnp.where(allowed, scores, masked_fill_value)
    return (scores, allowed, key_rows, value_rows)


def shards(
    tokens,
    cotangent,
    lengths,
    first_gain,
    joint_matrix,
    query_gain,
    key_gain,
    out_weight,
    second_gain,
    expand_weight,
    contract_weight,
):
    stretch_factor = tokens.shape[1]
    place = lax.axis_index("ctx")
    span = stretch_factor * lax.axis_size("ctx")
    slot_length_value = lengths[0]
    positions = place * stretch_factor + jnp.arange(stretch_factor, dtype=jnp.int32)
    valid = (positions < slot_length_value).astype(jnp.float32)[:, None]
    context_block_count = jnp.minimum(place, (slot_length_value - 1) // stretch_factor) + 1
    query_span_width = QUERY_HEADS * HEAD_SIZE
    key_span_width = KEY_VALUE_HEADS * HEAD_SIZE
    head_group = QUERY_HEADS // KEY_VALUE_HEADS
    scale = HEAD_SIZE ** (-0.5)
    gain_one, joint_full, query_scale, key_scale, out_full = (
        lax.all_gather(first_gain, "fsdp", axis=0, tiled=True),
        lax.all_gather(joint_matrix, "fsdp", axis=0, tiled=True),
        lax.all_gather(query_gain, "fsdp", axis=0, tiled=True),
        lax.all_gather(key_gain, "fsdp", axis=0, tiled=True),
        lax.all_gather(out_weight, "fsdp", axis=0, tiled=True),
    )
    rows = tokens[0].astype(jnp.float32)
    normed_one, inverse_one = rms_parts(rows)
    entry_one = (normed_one * gain_one.astype(jnp.float32)).astype(jnp.bfloat16)
    joint_projection = jnp.dot(entry_one, joint_full, preferred_element_type=jnp.float32)
    query_raw = joint_projection[:, :query_span_width].reshape(
        stretch_factor, QUERY_HEADS, HEAD_SIZE
    )
    unnormed_key = joint_projection[
        :, query_span_width : query_span_width + key_span_width
    ].reshape(stretch_factor, KEY_VALUE_HEADS, HEAD_SIZE)
    value_part = joint_projection[:, query_span_width + key_span_width :]
    cosine_table, sine_table = tables(positions, HEAD_SIZE)
    query_normed, query_inverse = rms_parts(query_raw)
    rotated_query = rotate(
        query_normed * query_scale.astype(jnp.float32), cosine_table, sine_table
    ).astype(jnp.bfloat16)
    key_normed, key_inverse = rms_parts(unnormed_key)
    key_rot = rotate(key_normed * key_scale.astype(jnp.float32), cosine_table, sine_table).astype(
        jnp.bfloat16
    )
    local_pair = jnp.concatenate(
        [key_rot.reshape(stretch_factor, key_span_width), value_part.astype(jnp.bfloat16)], axis=1
    )
    pair_all = lax.all_gather(local_pair, "ctx", axis=0, tiled=True)
    grouped_query = rotated_query.reshape(stretch_factor, KEY_VALUE_HEADS, head_group, HEAD_SIZE)

    def largest_step(index, carry):
        running, total = carry
        scores, allowed, key_rows, value_rows = block_scores(
            grouped_query,
            pair_all,
            index * stretch_factor,
            positions,
            slot_length_value,
            stretch_factor,
        )
        newer = jnp.maximum(running, jnp.max(scores, axis=-1))
        total = total * jnp.exp(running - newer) + jnp.sum(
            jnp.exp(scores - newer[..., None]), axis=-1
        )
        return (newer, total)

    largest_start = jnp.full(
        (KEY_VALUE_HEADS, head_group, stretch_factor), masked_fill_value, jnp.float32
    )
    running, total = lax.fori_loop(
        0,
        context_block_count,
        largest_step,
        (largest_start, jnp.zeros((KEY_VALUE_HEADS, head_group, stretch_factor), jnp.float32)),
    )
    log_total = running + jnp.log(total)

    def value_step(index, carry):
        rounded, exact = carry
        scores, allowed, key_rows, value_rows = block_scores(
            grouped_query,
            pair_all,
            index * stretch_factor,
            positions,
            slot_length_value,
            stretch_factor,
        )
        shares = jnp.where(allowed, jnp.exp(scores - log_total[..., None]), 0.0)
        rounded = rounded + jnp.einsum(
            "grqk,kgd->qgrd",
            shares.astype(jnp.bfloat16),
            value_rows,
            preferred_element_type=jnp.float32,
        )
        exact = exact + jnp.einsum(
            "grqk,kgd->qgrd",
            shares,
            value_rows.astype(jnp.float32),
            precision=lax.Precision.HIGHEST,
        )
        return (rounded, exact)

    blank_group = jnp.zeros((stretch_factor, KEY_VALUE_HEADS, head_group, HEAD_SIZE), jnp.float32)
    rounded, exact = lax.fori_loop(0, context_block_count, value_step, (blank_group, blank_group))
    mixed_output = rounded.reshape(stretch_factor, query_span_width).astype(jnp.bfloat16)
    hidden = rows + jnp.dot(mixed_output, out_full, preferred_element_type=jnp.float32)
    gain_two, expand_full, contract_full = (
        lax.all_gather(second_gain, "fsdp", axis=0, tiled=True),
        lax.all_gather(expand_weight, "fsdp", axis=0, tiled=True),
        lax.all_gather(contract_weight, "fsdp", axis=0, tiled=True),
    )
    normed_two, inverse_two = rms_parts(hidden)
    entry_two = (normed_two * gain_two.astype(jnp.float32)).astype(jnp.bfloat16)
    expanded = jnp.dot(entry_two, expand_full, preferred_element_type=jnp.float32)
    gate = expanded[:, :FF]
    upward = expanded[:, FF:]
    sigma = jax.nn.sigmoid(gate)
    activated = gate * sigma
    product = (activated * upward).astype(jnp.bfloat16)
    branch_two = jnp.dot(product, contract_full, preferred_element_type=jnp.float32)
    layer_output = ((hidden + branch_two) * valid).astype(jnp.bfloat16)
    gain_two, expand_full, contract_full = (
        lax.all_gather(second_gain, "fsdp", axis=0, tiled=True),
        lax.all_gather(expand_weight, "fsdp", axis=0, tiled=True),
        lax.all_gather(contract_weight, "fsdp", axis=0, tiled=True),
    )
    upstream = cotangent[0].astype(jnp.float32) * valid
    upstream_b = upstream.astype(jnp.bfloat16)
    contract_grad = cross_product(product, upstream_b)
    back_product = against(upstream_b, contract_full)
    grad_gate = back_product * upward * sigma * (1.0 + gate * (1.0 - sigma))
    grad_upward = back_product * activated
    grad_expanded = jnp.concatenate([grad_gate, grad_upward], axis=1).astype(jnp.bfloat16)
    expand_grad = cross_product(entry_two, grad_expanded)
    back_entry_two = against(grad_expanded, expand_full)
    second_grad = jnp.sum(back_entry_two * normed_two, axis=0)
    back_hidden = upstream + rms_back(
        back_entry_two * gain_two.astype(jnp.float32), normed_two, inverse_two
    )
    second_owned, expand_owned, contract_owned = (
        lax.psum_scatter(second_grad, "fsdp", scatter_dimension=0, tiled=True),
        lax.psum_scatter(expand_grad, "fsdp", scatter_dimension=0, tiled=True),
        lax.psum_scatter(contract_grad, "fsdp", scatter_dimension=0, tiled=True),
    )
    gain_one, joint_full, query_scale, key_scale, out_full = (
        lax.all_gather(first_gain, "fsdp", axis=0, tiled=True),
        lax.all_gather(joint_matrix, "fsdp", axis=0, tiled=True),
        lax.all_gather(query_gain, "fsdp", axis=0, tiled=True),
        lax.all_gather(key_gain, "fsdp", axis=0, tiled=True),
        lax.all_gather(out_weight, "fsdp", axis=0, tiled=True),
    )
    back_hidden_b = back_hidden.astype(jnp.bfloat16)
    out_grad = cross_product(mixed_output, back_hidden_b)
    mixed_backward = against(back_hidden_b, out_full).astype(jnp.bfloat16)
    group_backward = mixed_backward.reshape(stretch_factor, KEY_VALUE_HEADS, head_group, HEAD_SIZE)
    offset = jnp.transpose(jnp.sum(group_backward.astype(jnp.float32) * exact, axis=-1), (1, 2, 0))
    pair_all = lax.all_gather(local_pair, "ctx", axis=0, tiled=True)

    def grad_step(index, carry):
        grad_query, pair_grads = carry
        start = index * stretch_factor
        scores, allowed, key_rows, value_rows = block_scores(
            grouped_query, pair_all, start, positions, slot_length_value, stretch_factor
        )
        shares = jnp.where(allowed, jnp.exp(scores - log_total[..., None]), 0.0)
        back_shares = jnp.einsum(
            "qgrd,kgd->grqk", group_backward, value_rows, preferred_element_type=jnp.float32
        )
        back_scores = (shares * (back_shares - offset[..., None])).astype(jnp.bfloat16)
        grad_query = grad_query + jnp.einsum(
            "grqk,kgd->qgrd", back_scores, key_rows, preferred_element_type=jnp.float32
        )
        grad_keys = (
            jnp.einsum(
                "grqk,qgrd->kgd", back_scores, grouped_query, preferred_element_type=jnp.float32
            )
            * scale
        )
        grad_values = jnp.einsum(
            "grqk,qgrd->kgd",
            shares.astype(jnp.bfloat16),
            group_backward,
            preferred_element_type=jnp.float32,
        )
        block_grad = jnp.concatenate(
            [
                grad_keys.reshape(stretch_factor, key_span_width),
                grad_values.reshape(stretch_factor, key_span_width),
            ],
            axis=1,
        )
        pair_grads = lax.dynamic_update_slice_in_dim(pair_grads, block_grad, start, 0)
        return (grad_query, pair_grads)

    grad_query, pair_grads = lax.fori_loop(
        0,
        context_block_count,
        grad_step,
        (blank_group, jnp.zeros((span, 2 * key_span_width), jnp.float32)),
    )
    local_pairing = lax.psum_scatter(pair_grads, "ctx", scatter_dimension=0, tiled=True)
    back_query_rot = reverse_rotation(
        grad_query.reshape(stretch_factor, QUERY_HEADS, HEAD_SIZE) * scale, cosine_table, sine_table
    )
    query_gain_grad = jnp.sum(back_query_rot * query_normed, axis=(0, 1))
    grad_query_raw = rms_back(
        back_query_rot * query_scale.astype(jnp.float32), query_normed, query_inverse
    )
    rotated_key_backward = reverse_rotation(
        local_pairing[:, :key_span_width].reshape(stretch_factor, KEY_VALUE_HEADS, HEAD_SIZE),
        cosine_table,
        sine_table,
    )
    key_gain_grad = jnp.sum(rotated_key_backward * key_normed, axis=(0, 1))
    grad_key_raw = rms_back(
        rotated_key_backward * key_scale.astype(jnp.float32), key_normed, key_inverse
    )
    grad_joint = jnp.concatenate(
        [
            grad_query_raw.reshape(stretch_factor, query_span_width),
            grad_key_raw.reshape(stretch_factor, key_span_width),
            local_pairing[:, key_span_width:],
        ],
        axis=1,
    ).astype(jnp.bfloat16)
    joint_grad = cross_product(entry_one, grad_joint)
    back_entry_one = against(grad_joint, joint_full)
    first_grad = jnp.sum(back_entry_one * normed_one, axis=0)
    input_gradient = back_hidden + rms_back(
        back_entry_one * gain_one.astype(jnp.float32), normed_one, inverse_one
    )
    first_owned, joint_owned, query_owned, key_owned, out_owned = (
        lax.psum_scatter(first_grad, "fsdp", scatter_dimension=0, tiled=True),
        lax.psum_scatter(joint_grad, "fsdp", scatter_dimension=0, tiled=True),
        lax.psum_scatter(query_gain_grad, "fsdp", scatter_dimension=0, tiled=True),
        lax.psum_scatter(key_gain_grad, "fsdp", scatter_dimension=0, tiled=True),
        lax.psum_scatter(out_grad, "fsdp", scatter_dimension=0, tiled=True),
    )
    summed = lax.psum(
        (
            first_owned,
            joint_owned,
            query_owned,
            key_owned,
            out_owned,
            second_owned,
            expand_owned,
            contract_owned,
        ),
        ("ctx", "rep"),
    )
    return (layer_output[None], input_gradient[None]) + tuple(summed)


def solution(mesh):
    return jax.shard_map(
        shards,
        mesh=mesh,
        in_specs=(
            P(("fsdp", "rep"), "ctx", None),
            P(("fsdp", "rep"), "ctx", None),
            P(("fsdp", "rep")),
            P("fsdp"),
            P("fsdp", None),
            P("fsdp"),
            P("fsdp"),
            P("fsdp", None),
            P("fsdp"),
            P("fsdp", None),
            P("fsdp", None),
        ),
        out_specs=(
            P(("fsdp", "rep"), "ctx", None),
            P(("fsdp", "rep"), "ctx", None),
            P("fsdp"),
            P("fsdp", None),
            P("fsdp"),
            P("fsdp"),
            P("fsdp", None),
            P("fsdp"),
            P("fsdp", None),
            P("fsdp", None),
        ),
        check_vma=False,
    )
```

profile of v0, /device:TPU:0, one launch (start us, length us, event | category | flops | bytes accessed | tf_op | source)
XLA Modules:
  0.0 4372.1 jit_solution(18229859901072036340)
XLA Ops:
  10.8 13.5 all-gather
  26.1 12.9 all-reduce.10
  39.1 13.1 all-gather.1
  52.7 101.0 %all-gather.7.cloned.1.call-done = bf16[2048,1920]{1,0:T(8,128)(2,1)} async-done(((bf16[512,1920]{1,0:T(8,128)(2,1)}), bf16[2048,1920]{1,0:T(8,128)(2,1)}) %all-gather.7.cloned.1.call-update) | async-done | bytes 7864336 | tf_op jit(solution)/shard_map/all_gather | solution.py:103
  153.7 4.5 fusion.59
  160.3 6.8 all_gather.39
  172.6 4.4 while.40
  177.0 74.6 %all-gather.9.cloned.1.call-done = bf16[1280,2048]{1,0:T(8,128)(2,1)} async-done(((bf16[320,2048]{1,0:T(8,128)(2,1)}), bf16[1280,2048]{1,0:T(8,128)(2,1)}) %all-gather.9.cloned.1.call-update) | async-done | bytes 5242896 | tf_op jit(solution)/shard_map/all_gather | solution.py:106
  251.7 3.4 multiply_reduce_fusion.2
  255.2 696.3 %all-gather.11.cloned.1.call-done = bf16[2048,10240]{1,0:T(8,128)(2,1)} async-done(((bf16[512,10240]{1,0:T(8,128)(2,1)}), bf16[2048,10240]{1,0:T(8,128)(2,1)}) %all-gather.11.cloned.1.call-update) | async-done | bytes 41943056 | tf_op jit(solution)/shard_map/all_gather | solution.py:192
  951.5 21.9 fusion.64
  973.4 334.6 %all-gather.13.cloned.1.call-done = bf16[5120,2048]{1,0:T(8,128)(2,1)} async-done(((bf16[1280,2048]{1,0:T(8,128)(2,1)}), bf16[5120,2048]{1,0:T(8,128)(2,1)}) %all-gather.13.cloned.1.call-update) | async-done | bytes 20971536 | tf_op jit(solution)/shard_map/all_gather | solution.py:193
  1308.0 13.6 multiply_convert_fusion.1
  1321.6 20.5 multiply_reduce_fusion
  1343.5 4.3 convolution_convert_fusion
  1349.7 6.1 while.41
  1355.9 6.9 fusion.48
  1379.8 8.5 fusion.57
  1389.6 17.5 fusion.51
  1407.3 30.9 fusion.32
  1438.3 119.1 %reduce-scatter.12.cloned.1.call-done = f32[320,2048]{1,0:T(8,128)} async-done(((f32[1280,2048]{1,0:T(8,128)}), f32[320,2048]{1,0:T(8,128)}) %reduce-scatter.12.cloned.1.call-update) | async-done | bytes 2621456 | tf_op jit(solution)/shard_map/reduce_scatter | solution.py:320
  1557.5 266.8 %reduce-scatter.10.cloned.1.call-done = f32[512,1920]{1,0:T(8,128)} async-done(((f32[2048,1920]{1,0:T(8,128)}), f32[512,1920]{1,0:T(8,128)}) %reduce-scatter.10.cloned.1.call-update) | async-done | bytes 3932176 | tf_op jit(solution)/shard_map/reduce_scatter | solution.py:317
  1824.2 689.9 %reduce-scatter.14.cloned.1.call-done = f32[1280,2048]{1,0:T(8,128)} async-done(((f32[5120,2048]{1,0:T(8,128)}), f32[1280,2048]{1,0:T(8,128)}) %reduce-scatter.14.cloned.1.call-update) | async-done | bytes 10485776 | tf_op jit(solution)/shard_map/reduce_scatter | solution.py:226
  2514.1 1368.5 %reduce-scatter.16.cloned.1.call-done = f32[512,10240]{1,0:T(8,128)} async-done(((f32[2048,10240]{1,0:T(8,128)}), f32[512,10240]{1,0:T(8,128)}) %reduce-scatter.16.cloned.1.call-update) | async-done | bytes 20971536
  3885.8 10.7 fusion.31
  3896.8 6.1 fusion.44
  3902.9 19.1 all-reduce.9
  3922.2 13.2 all-reduce.7
  3936.8 400.2 %all-reduce.13.cloned.1.call-done = (f32[512,1920]{1,0:T(8,128)}, f32[320,2048]{1,0:T(8,128)}, f32[512,10240]{1,0:T(8,128)}, f32[1280,2048]{1,0:T(8,128)}) async-done(((f32[512,1920]{1,0:T(8,128)}, f32[320,2048]{1,0:T(8,128)}, f32[512,10240]{1,0:T(8,128)}, f32[1280,2048]{1,0:T(8,128)}), (f32[512,1920]{1,0:T(8,128)}, f32[320,2048]{1,0:T(8,128)}, f32[512,10240]{1,0:T(8,128)}, ...) | async-done | bytes 38010896 | tf_op jit(solution)/shard_map/psum | solution.py:322
  4337.0 4.4 copy.197
  4343.0 18.0 copy.199
  4361.0 4.1 copy.200
  (230 shorter events, 50.6 us)
Async XLA Ops:
  7.2 146.6 %all-gather.7.cloned.1.call-start = ((), (), s32[]{:S(2)}) async-start(), calls=%async_computation.5 | async-start | bytes 9830400 | tf_op jit(solution)/shard_map/all_gather | solution.py:103
  7.9 243.8 %all-gather.9.cloned.1.call-start = ((), (), s32[]{:S(2)}) async-start(), calls=%async_computation.6 | async-start | bytes 6553600 | tf_op jit(solution)/shard_map/all_gather | solution.py:106
  8.7 942.8 %all-gather.11.cloned.1.call-start = ((), (), s32[]{:S(2)}) async-start(), calls=%async_computation.7 | async-start | bytes 52428800 | tf_op jit(solution)/shard_map/all_gather | solution.py:192
  9.4 15.0 copy-start.35
  9.4 16.2 copy-start.43
  9.4 16.5 copy-start.44
  9.4 29.7 copy-start.38
  9.4 42.9 copy-start
  9.5 1298.5 %all-gather.13.cloned.1.call-start = ((), (), s32[]{:S(2)}) async-start(), calls=%async_computation.8 | async-start | bytes 26214400 | tf_op jit(solution)/shard_map/all_gather | solution.py:193
  10.0 1366.5 %reduce-scatter.8.cloned.1.call-start = ((), (), s32[]{:S(2)}) async-start(), calls=%async_computation.9 | async-start | bytes 983040 | tf_op jit(solution)/shard_map/reduce_scatter | solution.py:284
  39.1 13.2 copy-start.39
  39.1 119.2 %copy-start.41 = (bf16[64]{0:T(256)(128)(2,1)}, bf16[64]{0:T(256)(128)(2,1)S(1)}, u32[]{:S(2)}) copy-start(bf16[64]{0:T(256)(128)(2,1)S(1)} %get-tuple-element.449) | copy-start | bytes 388
  39.1 120.4 %copy-start.31 = (f32[64]{0:T(128)}, f32[64]{0:T(128)S(1)}, u32[]{:S(2)}) copy-start(f32[64]{0:T(128)S(1)} %convert_element_type.96) | copy-start | bytes 772
  39.1 129.2 %copy-start.33 = (f32[64]{0:T(128)}, f32[64]{0:T(128)S(1)}, u32[]{:S(2)}) copy-start(f32[64]{0:T(128)S(1)} %convert_element_type.99) | copy-start | bytes 772
  52.3 1289.8 %copy-start.30 = (f32[128]{0:T(128)}, f32[128]{0:T(128)S(1)}, u32[]{:S(2)}) copy-start(f32[128]{0:T(128)S(1)} %compare_convert_fusion) | copy-start | bytes 1540
  52.5 105.7 %copy-start.26 = (f32[128]{0:T(128)}, f32[128]{0:T(128)S(1)}, u32[]{:S(2)}) copy-start(f32[128]{0:T(128)S(1)} %add_rsqrt_fusion.3) | copy-start | bytes 1540
  52.7 116.6 %copy-start.15 = (f32[128,32]{0,1:T(8,128)}, f32[128,32]{0,1:T(8,128)S(1)}, u32[]{:S(2)}) copy-start(f32[128,32]{0,1:T(8,128)S(1)} %get-tuple-element.481) | copy-start | bytes 49156
  52.7 116.6 %copy-start.17 = (f32[128,32]{0,1:T(8,128)}, f32[128,32]{0,1:T(8,128)S(1)}, u32[]{:S(2)}) copy-start(f32[128,32]{0,1:T(8,128)S(1)} %get-tuple-element.482) | copy-start | bytes 49156
  177.0 78.1 %copy-start.10 = (bf16[128,5,4,64]{0,3,2,1:T(8,128)(2,1)}, bf16[128,5,4,64]{0,3,2,1:T(8,128)(2,1)S(1)}, u32[]{:S(2)}) copy-start(bf16[128,5,4,64]{0,3,2,1:T(8,128)(2,1)S(1)} %convert_element_type.100) | copy-start | bytes 983044
  255.2 1086.9 %copy-start.23 = (f32[128]{0:T(128)}, f32[128]{0:T(128)S(1)}, u32[]{:S(2)}) copy-start(f32[128]{0:T(128)S(1)} %add_rsqrt_fusion.2) | copy-start | bytes 1540
  951.5 356.5 %copy-start.12 = (bf16[1,128,2048]{2,1,0:T(8,128)(2,1)S(1)}, bf16[1,128,2048]{2,1,0:T(8,128)(2,1)}, u32[]{:S(2)}) copy-start(bf16[1,128,2048]{2,1,0:T(8,128)(2,1)} %param.18) | copy-start | bytes 1572868
  1355.9 201.6 %reduce-scatter.12.cloned.1.call-start = ((), (), s32[]{:S(2)}) async-start(), calls=%async_computation.11 | async-start | bytes 13107200 | tf_op jit(solution)/shard_map/reduce_scatter | solution.py:320
  1362.9 461.3 %reduce-scatter.10.cloned.1.call-start = ((), (), s32[]{:S(2)}) async-start(), calls=%async_computation.10 | async-start | bytes 19660800 | tf_op jit(solution)/shard_map/reduce_scatter | solution.py:317
  1388.3 1125.8 %reduce-scatter.14.cloned.1.call-start = ((), (), s32[]{:S(2)}) async-start(), calls=%async_computation.12 | async-start | bytes 52428800 | tf_op jit(solution)/shard_map/reduce_scatter | solution.py:226
  1407.1 2475.5 %reduce-scatter.16.cloned.1.call-start = ((), (), s32[]{:S(2)}) async-start(), calls=%async_computation.13 | async-start | bytes 104857600
  1438.3 2898.8 %all-reduce.13.cloned.1.call-start = ((), (), s32[]{:S(2)}) async-start(), calls=%async_computation.14 | async-start | bytes 76021760 | tf_op jit(solution)/shard_map/psum | solution.py:322
  3885.8 10.7 copy-start.14
  3885.8 10.9 copy-start.28
  3896.8 38.7 copy-start.2
  4341.5 19.5 slice-start
  4343.0 18.0 slice-start.1
  4343.0 18.0 slice-start.2
  (26 other events, 95.3 us)
Sparse Core Ops, SparseCore 0:
  9.6 144.1 all-gather.6
  155.3 96.3 all-gather.8
  253.3 698.1 all-gather.10
  952.9 355.0 all-gather.12
  1356.0 20.4 reduce-scatter.7
  1379.4 177.9 reduce-scatter.11
  1560.5 263.6 reduce-scatter.9
  1826.7 687.3 reduce-scatter.13
  2516.5 1366.0 reduce-scatter.15
  3887.2 449.7 all-reduce.12
where the time goes:
time: 4380 us; the launch traced here: 4370 us
  waiting for transfers between devices  4060 us (93%)
  matrix products  155 us (4%)
  blocking collectives  78.7 us (2%)
  local copies, waits for them, and re-layouts  51 us (1%)
    unnamed x11, waiting for transfers between devices  1370 us
    all_gather x1, waiting for transfers between devices, shards(): lax.all_gather(expand_weight, 'fsdp', axis=0, tiled=True)  696 us
    reduce_scatter x1, waiting for transfers between devices, shards(): lax.psum_scatter(contract_grad, 'fsdp', scatter_dimension=0, tiled=True)  690 us
    psum x1, waiting for transfers between devices, shards(): lax.psum((first_owned, joint_owned, query_owned, key_owned, out_owned, se...  400 us
    all_gather x1, waiting for transfers between devices, shards(): lax.all_gather(contract_weight, 'fsdp', axis=0, tiled=True)  335 us
    reduce_scatter x1, waiting for transfers between devices, shards(): lax.psum_scatter(joint_grad, 'fsdp', scatter_dimension=0, tiled=True)  267 us
    reduce_scatter x1, waiting for transfers between devices, shards(): lax.psum_scatter(out_grad, 'fsdp', scatter_dimension=0, tiled=True)  119 us
    all_gather x1, waiting for transfers between devices, shards(): lax.all_gather(joint_matrix, 'fsdp', axis=0, tiled=True)  101 us
  transfers between devices with their start and end apart: 10, of which 10 were waited for; matrix products, arithmetic and copies ran while one was open for 3% of the time, Pallas kernels for 0%

commit v1 on v0

--- a/solution.py
+++ b/solution.py
@@ -10,6 +10,24 @@
 FF = 5120
 epsilon = 1e-06
 masked_fill_value = -1e30
+
+
+def collect(shard, axis, dim):
+    ways, here, hop = (lax.axis_size(axis), lax.axis_index(axis), shard.shape[dim])
+    dims = [n * ways if d == dim else n for d, n in enumerate(shard.shape)]
+    full = lax.dynamic_update_slice_in_dim(
+        jnp.zeros(dims, shard.dtype), shard, here * hop, axis=dim
+    )
+    going_up = going_down = shard
+    for far in range(1, ways // 2 + 1):
+        going_up = lax.ppermute(going_up, axis, [(d, (d + 1) % ways) for d in range(ways)])
+        full = lax.dynamic_update_slice_in_dim(full, going_up, (here - far) % ways * hop, axis=dim)
+        if 2 * far < ways:
+            going_down = lax.ppermute(going_down, axis, [(d, (d - 1) % ways) for d in range(ways)])
+            full = lax.dynamic_update_slice_in_dim(
+                full, going_down, (here + far) % ways * hop, axis=dim
+            )
+    return full
 
 
 def tables(positions, width):
@@ -190,7 +208,7 @@
     gain_two, expand_full, contract_full = (
         lax.all_gather(second_gain, "fsdp", axis=0, tiled=True),
         lax.all_gather(expand_weight, "fsdp", axis=0, tiled=True),
-        lax.all_gather(contract_weight, "fsdp", axis=0, tiled=True),
+        collect(contract_weight, "fsdp", 0),
     )
     normed_two, inverse_two = rms_parts(hidden)
     entry_two = (normed_two * gain_two.astype(jnp.float32)).astype(jnp.bfloat16)

time: 4380 us -> 4380 us (level)
  waiting for transfers between devices: 4060 us -> 3910 us
  starting transfers between devices: 0.61 us -> 116 us
    psum x1, waiting for transfers between devices: 400 us -> 54.2 us  [shards(): lax.psum((first_owned, joint_owned, query_owned, key_owned, out_owned, se...]
    ppermute x0 -> x3, waiting for transfers between devices: none -> 202 us  [the longest x2 202 us: collect(): lax.ppermute(going_up, axis, [(d, (d + 1) % ways) for d in range(ways)])]
    ppermute x0 -> x3, starting transfers between devices: none -> 115 us  [the longest x2 111 us: collect(): lax.ppermute(going_up, axis, [(d, (d + 1) % ways) for d in range(ways)])]
  transfers between devices with their start and end apart: 10 -> 13, of which waited for: 10 -> 12; matrix products, arithmetic and copies ran while one was open for 3% -> 4% of each run, Pallas kernels for 0% -> 0%
where the time goes in v1:
time: 4380 us; the launch traced here: 4370 us
  waiting for transfers between devices  3910 us (89%)
  matrix products  156 us (4%)
  starting transfers between devices  116 us (3%)
  local copies, waits for them, and re-layouts  81.6 us (2%)
  blocking collectives  76.7 us (2%)
    unnamed x11, waiting for transfers between devices  1370 us
    all_gather x1, waiting for transfers between devices, shards(): lax.all_gather(expand_weight, 'fsdp', axis=0, tiled=True)  696 us
    reduce_scatter x1, waiting for transfers between devices, shards(): lax.psum_scatter(contract_grad, 'fsdp', scatter_dimension=0, tiled=True)  690 us
    all_gather x1, waiting for transfers between devices, shards(): lax.all_gather(contract_weight, 'fsdp', axis=0, tiled=True)  335 us
    reduce_scatter x1, waiting for transfers between devices, shards(): lax.psum_scatter(joint_grad, 'fsdp', scatter_dimension=0, tiled=True)  267 us
    ppermute x2, waiting for transfers between devices, collect(): lax.ppermute(going_up, axis, [(d, (d + 1) % ways) for d in range(ways)])  202 us
    reduce_scatter x1, waiting for transfers between devices, shards(): lax.psum_scatter(out_grad, 'fsdp', scatter_dimension=0, tiled=True)  119 us
    ppermute x2, starting transfers between devices, collect(): lax.ppermute(going_up, axis, [(d, (d + 1) % ways) for d in range(ways)])  111 us
  transfers between devices with their start and end apart: 13, of which 12 were waited for; matrix products, arithmetic and copies ran while one was open for 4% of the time, Pallas kernels for 0%

profile of v1, /device:TPU:0, one launch (start us, length us, event | category | flops | bytes accessed | tf_op | source)
XLA Modules:
  0.0 4372.1 jit_solution(14978836218572980852)
XLA Ops:
  10.8 13.5 all-gather
  26.1 12.9 all-reduce.10
  39.1 13.1 all-gather.1
  52.7 101.0 %all-gather.7.cloned.1.call-done = bf16[2048,1920]{1,0:T(8,128)(2,1)} async-done(((bf16[512,1920]{1,0:T(8,128)(2,1)}), bf16[2048,1920]{1,0:T(8,128)(2,1)}) %all-gather.7.cloned.1.call-update) | async-done | bytes 7864336 | tf_op jit(solution)/shard_map/all_gather | solution.py:121
  159.0 6.8 all_gather.38
  175.5 76.2 %all-gather.9.cloned.1.call-done = bf16[1280,2048]{1,0:T(8,128)(2,1)} async-done(((bf16[320,2048]{1,0:T(8,128)(2,1)}), bf16[1280,2048]{1,0:T(8,128)(2,1)}) %all-gather.9.cloned.1.call-update) | async-done | bytes 5242896 | tf_op jit(solution)/shard_map/all_gather | solution.py:124
  255.2 696.3 %all-gather.11.cloned.1.call-done = bf16[2048,10240]{1,0:T(8,128)(2,1)} async-done(((bf16[512,10240]{1,0:T(8,128)(2,1)}), bf16[2048,10240]{1,0:T(8,128)(2,1)}) %all-gather.11.cloned.1.call-update) | async-done | bytes 41943056 | tf_op jit(solution)/shard_map/all_gather | solution.py:210
  951.5 21.9 fusion.64
  973.4 334.6 %all-gather.13.cloned.1.call-done = bf16[5120,2048]{1,0:T(8,128)(2,1)} async-done(((bf16[1280,2048]{1,0:T(8,128)(2,1)}), bf16[5120,2048]{1,0:T(8,128)(2,1)}) %all-gather.13.cloned.1.call-update) | async-done | bytes 20971536 | tf_op jit(solution)/shard_map/all_gather | solution.py:226
  1308.0 13.6 multiply_convert_fusion.1
  1321.6 20.5 multiply_reduce_fusion
  1349.7 6.1 while.41
  1355.9 6.9 fusion.48
  1379.9 8.5 fusion.57
  1389.7 17.5 fusion.51
  1407.8 30.9 fusion.32
  1438.8 118.7 %reduce-scatter.12.cloned.1.call-done = f32[320,2048]{1,0:T(8,128)} async-done(((f32[1280,2048]{1,0:T(8,128)}), f32[320,2048]{1,0:T(8,128)}) %reduce-scatter.12.cloned.1.call-update) | async-done | bytes 2621456 | tf_op jit(solution)/shard_map/reduce_scatter | solution.py:338
  1557.4 266.8 %reduce-scatter.10.cloned.1.call-done = f32[512,1920]{1,0:T(8,128)} async-done(((f32[2048,1920]{1,0:T(8,128)}), f32[512,1920]{1,0:T(8,128)}) %reduce-scatter.10.cloned.1.call-update) | async-done | bytes 3932176 | tf_op jit(solution)/shard_map/reduce_scatter | solution.py:335
  1824.2 689.9 %reduce-scatter.14.cloned.1.call-done = f32[1280,2048]{1,0:T(8,128)} async-done(((f32[5120,2048]{1,0:T(8,128)}), f32[1280,2048]{1,0:T(8,128)}) %reduce-scatter.14.cloned.1.call-update) | async-done | bytes 10485776 | tf_op jit(solution)/shard_map/reduce_scatter | solution.py:244
  2514.1 1368.5 %reduce-scatter.16.cloned.1.call-done = f32[512,10240]{1,0:T(8,128)} async-done(((f32[2048,10240]{1,0:T(8,128)}), f32[512,10240]{1,0:T(8,128)}) %reduce-scatter.16.cloned.1.call-update) | async-done | bytes 20971536
  3886.4 114.2 %collective-permute-done = bf16[1280,2048]{1,0:T(8,128)(2,1)} collective-permute-done((bf16[1280,2048]{1,0:T(8,128)(2,1)}, bf16[1280,2048]{1,0:T(8,128)(2,1)}, u32[]{:S(2)}, u32[]{:S(2)}) %collective-permute-start) | collective-permute-done | bytes 5242912 | tf_op jit(solution)/shard_map/ppermute | solution.py:23
  4000.7 111.4 %collective-permute-start.2 = (bf16[1280,2048]{1,0:T(8,128)(2,1)}, bf16[1280,2048]{1,0:T(8,128)(2,1)}, u32[]{:S(2)}, u32[]{:S(2)}) collective-permute-start(bf16[1280,2048]{1,0:T(8,128)(2,1)} %collective-permute-done), channel_id=1, source_target_pairs={{0,4},{4,8},{8,12},{12,0},{1,5},{5,9},{9,13},{13,1},{2,6},{6,10},{... | collective-permute-start | bytes 15728648 | tf_op jit(solution)/shard_map/ppermute | solution.py:23
  4113.4 8.3 broadcast_in_dim.86
  4127.4 5.8 constant_dynamic-update-slice_fusion.3
  4133.2 6.0 constant_dynamic-update-slice_fusion.2
  4139.2 87.3 %collective-permute-done.2 = bf16[1280,2048]{1,0:T(8,128)(2,1)} collective-permute-done((bf16[1280,2048]{1,0:T(8,128)(2,1)}, bf16[1280,2048]{1,0:T(8,128)(2,1)}, u32[]{:S(2)}, u32[]{:S(2)}) %collective-permute-start.2) | collective-permute-done | bytes 5242912 | tf_op jit(solution)/shard_map/ppermute | solution.py:23
  4232.4 11.6 fusion.31
  4244.2 6.6 fusion.44
  4250.9 16.9 all-reduce.9
  4268.1 13.3 all-reduce.7
  4282.8 54.2 %all-reduce.13.cloned.1.call-done = (f32[512,1920]{1,0:T(8,128)}, f32[320,2048]{1,0:T(8,128)}, f32[512,10240]{1,0:T(8,128)}, f32[1280,2048]{1,0:T(8,128)}) async-done(((f32[512,1920]{1,0:T(8,128)}, f32[320,2048]{1,0:T(8,128)}, f32[512,10240]{1,0:T(8,128)}, f32[1280,2048]{1,0:T(8,128)}), (f32[512,1920]{1,0:T(8,128)}, f32[320,2048]{1,0:T(8,128)}, f32[512,10240]{1,0:T(8,128)}, ...) | async-done | bytes 38010896 | tf_op jit(solution)/shard_map/psum | solution.py:340
  4342.9 18.0 copy.203
  (239 shorter events, 88.3 us)
Async XLA Ops:
  7.2 146.6 %all-gather.7.cloned.1.call-start = ((), (), s32[]{:S(2)}) async-start(), calls=%async_computation.5 | async-start | bytes 9830400 | tf_op jit(solution)/shard_map/all_gather | solution.py:121
  7.9 243.8 %all-gather.9.cloned.1.call-start = ((), (), s32[]{:S(2)}) async-start(), calls=%async_computation.6 | async-start | bytes 6553600 | tf_op jit(solution)/shard_map/all_gather | solution.py:124
  8.7 942.8 %all-gather.11.cloned.1.call-start = ((), (), s32[]{:S(2)}) async-start(), calls=%async_computation.7 | async-start | bytes 52428800 | tf_op jit(solution)/shard_map/all_gather | solution.py:210
  9.4 16.2 copy-start.42
  9.4 16.5 copy-start.43
  9.4 29.7 copy-start.37
  9.4 42.9 copy-start
  9.5 1298.5 %all-gather.13.cloned.1.call-start = ((), (), s32[]{:S(2)}) async-start(), calls=%async_computation.8 | async-start | bytes 26214400 | tf_op jit(solution)/shard_map/all_gather | solution.py:226
  10.0 1366.4 %reduce-scatter.8.cloned.1.call-start = ((), (), s32[]{:S(2)}) async-start(), calls=%async_computation.9 | async-start | bytes 983040 | tf_op jit(solution)/shard_map/reduce_scatter | solution.py:302
  39.1 119.2 %copy-start.38 = (bf16[64]{0:T(256)(128)(2,1)}, bf16[64]{0:T(256)(128)(2,1)S(1)}, u32[]{:S(2)}) copy-start(bf16[64]{0:T(256)(128)(2,1)S(1)} %get-tuple-element.448) | copy-start | bytes 388
  39.1 119.2 %copy-start.40 = (bf16[64]{0:T(256)(128)(2,1)}, bf16[64]{0:T(256)(128)(2,1)S(1)}, u32[]{:S(2)}) copy-start(bf16[64]{0:T(256)(128)(2,1)S(1)} %get-tuple-element.449) | copy-start | bytes 388
  39.1 119.6 %copy-start.31 = (f32[64]{0:T(128)}, f32[64]{0:T(128)S(1)}, u32[]{:S(2)}) copy-start(f32[64]{0:T(128)S(1)} %convert_element_type.96) | copy-start | bytes 772
  39.1 128.0 %copy-start.33 = (f32[64]{0:T(128)}, f32[64]{0:T(128)S(1)}, u32[]{:S(2)}) copy-start(f32[64]{0:T(128)S(1)} %convert_element_type.99) | copy-start | bytes 772
  52.3 1289.8 %copy-start.29 = (f32[128]{0:T(128)}, f32[128]{0:T(128)S(1)}, u32[]{:S(2)}) copy-start(f32[128]{0:T(128)S(1)} %compare_convert_fusion) | copy-start | bytes 1540
  52.5 105.8 %copy-start.26 = (f32[128]{0:T(128)}, f32[128]{0:T(128)S(1)}, u32[]{:S(2)}) copy-start(f32[128]{0:T(128)S(1)} %add_rsqrt_fusion.3) | copy-start | bytes 1540
  52.7 114.6 %copy-start.14 = (f32[128,32]{0,1:T(8,128)}, f32[128,32]{0,1:T(8,128)S(1)}, u32[]{:S(2)}) copy-start(f32[128,32]{0,1:T(8,128)S(1)} %get-tuple-element.481) | copy-start | bytes 49156
  52.7 114.6 %copy-start.16 = (f32[128,32]{0,1:T(8,128)}, f32[128,32]{0,1:T(8,128)S(1)}, u32[]{:S(2)}) copy-start(f32[128,32]{0,1:T(8,128)S(1)} %get-tuple-element.482) | copy-start | bytes 49156
  175.5 79.7 %copy-start.11 = (bf16[128,5,4,64]{0,3,2,1:T(8,128)(2,1)}, bf16[128,5,4,64]{0,3,2,1:T(8,128)(2,1)S(1)}, u32[]{:S(2)}) copy-start(bf16[128,5,4,64]{0,3,2,1:T(8,128)(2,1)S(1)} %convert_element_type.100) | copy-start | bytes 983044
  255.2 1086.9 %copy-start.22 = (f32[128]{0:T(128)}, f32[128]{0:T(128)S(1)}, u32[]{:S(2)}) copy-start(f32[128]{0:T(128)S(1)} %add_rsqrt_fusion.2) | copy-start | bytes 1540
  951.5 356.5 %copy-start.13 = (bf16[1,128,2048]{2,1,0:T(8,128)(2,1)S(1)}, bf16[1,128,2048]{2,1,0:T(8,128)(2,1)}, u32[]{:S(2)}) copy-start(bf16[1,128,2048]{2,1,0:T(8,128)(2,1)} %param.18) | copy-start | bytes 1572868
  1355.8 201.6 %reduce-scatter.12.cloned.1.call-start = ((), (), s32[]{:S(2)}) async-start(), calls=%async_computation.11 | async-start | bytes 13107200 | tf_op jit(solution)/shard_map/reduce_scatter | solution.py:338
  1362.9 461.3 %reduce-scatter.10.cloned.1.call-start = ((), (), s32[]{:S(2)}) async-start(), calls=%async_computation.10 | async-start | bytes 19660800 | tf_op jit(solution)/shard_map/reduce_scatter | solution.py:335
  1388.4 1125.6 %reduce-scatter.14.cloned.1.call-start = ((), (), s32[]{:S(2)}) async-start(), calls=%async_computation.12 | async-start | bytes 52428800 | tf_op jit(solution)/shard_map/reduce_scatter | solution.py:244
  1407.2 2475.3 %reduce-scatter.16.cloned.1.call-start = ((), (), s32[]{:S(2)}) async-start(), calls=%async_computation.13 | async-start | bytes 104857600
  1438.7 2898.2 %all-reduce.13.cloned.1.call-start = ((), (), s32[]{:S(2)}) async-start(), calls=%async_computation.14 | async-start | bytes 76021760 | tf_op jit(solution)/shard_map/psum | solution.py:340
  3882.6 118.1 %collective-permute-start = (bf16[1280,2048]{1,0:T(8,128)(2,1)}, bf16[1280,2048]{1,0:T(8,128)(2,1)}, u32[]{:S(2)}, u32[]{:S(2)}) collective-permute-start(bf16[1280,2048]{1,0:T(8,128)(2,1)} %param.27), channel_id=1, source_target_pairs={{0,4},{4,8},{8,12},{12,0},{1,5},{5,9},{9,13},{13,1},{2,6},{6,10},{... | collective-permute-start | bytes 15728648 | tf_op jit(solution)/shard_map/ppermute | solution.py:23
  3882.6 250.6 %collective-permute-start.1 = (bf16[1280,2048]{1,0:T(8,128)(2,1)}, bf16[1280,2048]{1,0:T(8,128)(2,1)}, u32[]{:S(2)}, u32[]{:S(2)}) collective-permute-start(bf16[1280,2048]{1,0:T(8,128)(2,1)} %param.27), channel_id=1, source_target_pairs={{0,12},{4,0},{8,4},{12,8},{1,13},{5,1},{9,5},{13,9},{2,14},{6,2},{... | collective-permute-start | bytes 15728648 | tf_op jit(solution)/shard_map/ppermute | solution.py:26
  4000.7 225.9 %collective-permute-start.2 = (bf16[1280,2048]{1,0:T(8,128)(2,1)}, bf16[1280,2048]{1,0:T(8,128)(2,1)}, u32[]{:S(2)}, u32[]{:S(2)}) collective-permute-start(bf16[1280,2048]{1,0:T(8,128)(2,1)} %collective-permute-done), channel_id=1, source_target_pairs={{0,4},{4,8},{8,12},{12,0},{1,5},{5,9},{9,13},{13,1},{2,6},{6,10},{... | collective-permute-start | bytes 15728648 | tf_op jit(solution)/shard_map/ppermute | solution.py:23
  4244.2 37.2 copy-start.2
  4341.4 19.5 slice-start
  4342.9 18.0 slice-start.1
  4342.9 18.0 slice-start.2
  (28 other events, 129.8 us)
Sparse Core Ops, SparseCore 0:
  9.6 144.1 all-gather.6
  155.3 96.3 all-gather.8
  253.3 698.1 all-gather.10
  952.9 355.0 all-gather.12
  1356.0 20.4 reduce-scatter.7
  1379.4 177.9 reduce-scatter.11
  1560.5 263.6 reduce-scatter.9
  1826.7 687.3 reduce-scatter.13
  2516.4 1366.0 reduce-scatter.15
  3887.2 449.7 all-reduce.12
